TPU v7x, 32 devices: a whole 2x2x4 slice. The times are simulated.
32 devices in a mesh: grp: 4 (over z), mem: 8 (over y, x, core).
Axes of the slice: x: 2, y: 2, z: 4, core: 2. Of those that a mesh axis runs over, the one named last changes fastest.
Arguments:
- volume: float32 [4, 8, 8, 512, 1024], P('grp', 'mem'), may hold values from -1 to 1
- transfer_coef: float32 [4, 4], replicated, may hold values from -3 to 3
- group_order: int32 [4], replicated, may hold values from 0 to 3, each once
- member_order: int32 [4, 8], replicated, may hold values from 0 to 7, each once within a row
- active_mask: int32 [4, 8], P('grp', 'mem'), may hold values 0 or 1
Outputs:
- picture: float32 [4, 512, 1024], P(None, 'mem', 'grp')
All inputs are finite; a program needn't handle non-finite values. No bound on the sum of `active_mask` on one device may be relied on, other than what follows from the above.
Results may differ from a plain program's by a relative error of at most 0.0003.
Values sent between devices are 32-bit elements; how exact they have to be, the bound alone decides.
A program may use at most 192 MiB of HBM per device.

v0:
```python
import functools
import math

import jax
import jax.numpy as jnp
from jax import lax
from jax.experimental import pallas as pl
from jax.experimental.pallas import tpu as pltpu
from jax.sharding import PartitionSpec as P

MESH = pl.DeviceIdType.MESH
CHUNKS = 8
EARLY = 6
TILE_ROWS = 8


def kernel(groups, members, coef_ref, group_ref, member_ref, active_ref, volume_ref, out_ref,
           vol, tloc, tin, col, pcol, mout, min_, tnear, tslab, sout, sin, zout, zin,
           vol_sem, t_send, t_recv, c_send, c_recv, m_send, m_recv, s_send, s_recv, z_send, z_recv):
    chunks, _, samples, rows, cols = vol.shape
    block_rows = chunks * rows
    chips = members // 2
    group_cols = cols // groups
    g = lax.axis_index("grp")
    me = lax.axis_index("mem")
    chip = me // 2
    core = me % 2
    partner = me + 1 - 2 * core
    row_tiles = rows // TILE_ROWS

    def fetch(j, d):
        start = pl.multiple_of(d * block_rows + j * rows, TILE_ROWS)
        return pltpu.make_async_copy(
            volume_ref.at[0, 0, :, pl.ds(start, rows), :], vol.at[j, d], vol_sem.at[j])

    def send_t(j, d, src):
        return pltpu.make_async_remote_copy(
            tloc.at[j, d], tin.at[j, src], t_send, t_recv.at[j],
            device_id={"mem": d}, device_id_type=MESH)

    def send_col(j, k):
        return pltpu.make_async_remote_copy(
            col.at[j, 2 * k + 1 - core], pcol.at[j, k], c_send, c_recv.at[j],
            device_id={"mem": partner}, device_id_type=MESH)

    def send_m(j, k, src):
        return pltpu.make_async_remote_copy(
            mout.at[j, k], min_.at[j, src], m_send, m_recv.at[j],
            device_id={"mem": 2 * k + core}, device_id_type=MESH)

    def send_s(j, k, src):
        return pltpu.make_async_remote_copy(
            sout.at[j, k], sin.at[j, src], s_send, s_recv.at[j],
            device_id={"mem": 2 * k + core}, device_id_type=MESH)

    def send_z(j, k, src):
        return pltpu.make_async_remote_copy(
            zout.at[j, k], zin.at[j, src], z_send, z_recv.at[j],
            device_id={"grp": k}, device_id_type=MESH)

    def landed(ref, sem):
        pltpu.make_async_copy(ref, ref, sem).wait()

    def each(count, fn):
        def step(i, carry):
            fn(i)
            return carry
        lax.fori_loop(0, count, step, 0)

    each(chunks, lambda j: each(members, lambda off: fetch(j, (me + 1 + off) % members).start()))

    barrier = pltpu.get_barrier_semaphore()
    each(members - 1, lambda off: pl.semaphore_signal(
        barrier, inc=1, device_id={"mem": (me + 1 + off) % members}, device_id_type=MESH))
    each(groups - 1, lambda off: pl.semaphore_signal(
        barrier, inc=1, device_id={"grp": (g + 1 + off) % groups}, device_id_type=MESH))

    density_factor = math.sqrt(3.0 / (samples * groups * members) * math.log2(math.e))
    coef = [[coef_ref[c, p] * (0.5 if c < 3 else density_factor) for p in range(4)] for c in range(4)]
    active = active_ref[0, 0].astype(jnp.float32)
    half_active = active * 0.5
    width = min(512, cols)
    col_tiles = cols // width
    ranks = [member_ref[g, i] for i in range(members)]
    near = [jnp.minimum(ranks[2 * q], ranks[2 * q + 1]) for q in range(chips)]
    far = [jnp.maximum(ranks[2 * q], ranks[2 * q + 1]) for q in range(chips)]
    own_first = member_ref[g, me] < member_ref[g, partner]
    orders = [group_ref[i] for i in range(groups)]

    def tiles(fn, count=None):
        def step(i, carry):
            row = pl.ds(pl.multiple_of((i // col_tiles) * TILE_ROWS, TILE_ROWS), TILE_ROWS)
            column = pl.ds(pl.multiple_of((i % col_tiles) * width, width), width)
            fn(row, column)
            return carry
        lax.fori_loop(0, row_tiles * col_tiles, step, 0)

    def march(j, d):
        def tile(row, column):
            depth = jnp.zeros((TILE_ROWS, width), jnp.float32)
            light = jnp.ones((TILE_ROWS, width), jnp.float32)
            colour = [jnp.zeros((TILE_ROWS, width), jnp.float32) for _ in range(3)]
            for k in range(samples):
                v = vol[j, d, k, row, column]
                poly = [q[0] + v * (q[1] + v * (q[2] + v * q[3])) for q in coef]
                depth = depth - poly[3] * poly[3]
                after = jnp.exp2(depth)
                weight = light - after
                light = after
                colour = [colour[c] + weight * jnp.tanh(poly[c]) for c in range(3)]
            coverage = 1.0 - light
            tloc[j, d, row, column] = 1.0 - active * coverage
            for c in range(3):
                col[j, d, c, row, column] = half_active * (coverage + colour[c])
        tiles(tile)

    early = min(EARLY, members - 1)

    def produce(j):
        @pl.when(j > 0)
        def _():
            landed(vol.at[j], vol_sem.at[j])

        def unit(off):
            d = (me + 1 + off) % members

            @pl.when(jnp.logical_or(j > 0, off >= early))
            def _():
                march(j, d)

            @pl.when(off < members - 1)
            def _():
                send_t(j, d, me).start()

            @pl.when(d % 2 != core)
            def _():
                send_col(j, d // 2).start()
        each(members, unit)

        def keep(row, column):
            tin[j, me, row, column] = tloc[j, me, row, column]
        tiles(keep)

    def ratios(j):
        landed(tin.at[j, pl.ds(0, members - 1)], t_recv.at[j])

        def tile(row, column):
            t = [tin[j, i, row, column] for i in range(members)]
            total = t[0]
            for i in range(1, members):
                total = total * t[i]
            tslab[j, row, column] = total
            for q in range(chips):
                before = jnp.ones((TILE_ROWS, width), jnp.float32)
                between = jnp.ones((TILE_ROWS, width), jnp.float32)
                for i in range(members):
                    nearer = ranks[i] < near[q]
                    inside = jnp.logical_and(ranks[i] >= near[q], ranks[i] < far[q])
                    before = before * jnp.where(nearer, t[i], 1.0)
                    between = between * jnp.where(inside, t[i], 1.0)
                tnear[j, q, row, column] = before
                mout[j, q, row, column] = between
        tiles(tile)
        each(chips - 1, lambda off: send_m(j, (chip + 1 + off) % chips, chip).start())

        def keep(row, column):
            min_[j, chip, row, column] = mout[j, chip, row, column]
        tiles(keep)

    def pair_sums(j):
        landed(min_.at[j, pl.ds(0, chips - 1)], m_recv.at[j])
        landed(pcol.at[j], c_recv.at[j])

        def unit(off):
            k = (chip + 1 + off) % chips

            def tile(row, column):
                ratio = min_[j, k, row, column]
                own_factor = jnp.where(own_first, 1.0, ratio)
                other_factor = jnp.where(own_first, ratio, 1.0)
                for c in range(3):
                    sout[j, k, c, row, column] = (
                        col[j, 2 * k + core, c, row, column] * own_factor
                        + pcol[j, k, c, row, column] * other_factor)
            tiles(tile)

            @pl.when(off < chips - 1)
            def _():
                send_s(j, k, chip).start()
        each(chips, unit)

        def keep(row, column):
            for c in range(3):
                sin[j, chip, c, row, column] = sout[j, chip, c, row, column]
        tiles(keep)

    def slab(j):
        landed(sin.at[j, pl.ds(0, chips - 1)], s_recv.at[j])

        def part(k):
            def tile(i):
                row = pl.ds(pl.multiple_of(i * TILE_ROWS, TILE_ROWS), TILE_ROWS)
                column = pl.ds(pl.multiple_of(k * group_cols, group_cols), group_cols)
                factor = [tnear[j, q, row, column] for q in range(chips)]
                for c in range(3):
                    total = factor[0] * sin[j, 0, c, row, column]
                    for q in range(1, chips):
                        total = total + factor[q] * sin[j, q, c, row, column]
                    zout[j, k, c, row, :] = total
                zout[j, k, 3, row, :] = tslab[j, row, column]
            each(row_tiles, tile)

        def unit(off):
            k = (g + 1 + off) % groups
            part(k)

            @pl.when(off < groups - 1)
            def _():
                send_z(j, k, g).start()
        each(groups, unit)
        zin[j, g] = zout[j, g]

    def finish(j):
        landed(zin.at[j, pl.ds(0, groups - 1)], z_recv.at[j])
        for r in range(row_tiles):
            row = pl.ds(r * TILE_ROWS, TILE_ROWS)
            out_row = pl.ds(pl.multiple_of(j * rows + r * TILE_ROWS, TILE_ROWS), TILE_ROWS)
            t = [zin[j, i, 3, row, :] for i in range(groups)]
            total = t[0]
            for i in range(1, groups):
                total = total * t[i]
            out_ref[3, out_row, :] = 1.0 - total
            factor = []
            for i in range(groups):
                before = jnp.ones_like(total)
                for o in range(groups):
                    if o != i:
                        before = before * jnp.where(orders[o] < orders[i], t[o], 1.0)
                factor.append(before)
            for c in range(3):
                colour = factor[0] * zin[j, 0, c, row, :]
                for i in range(1, groups):
                    colour = colour + factor[i] * zin[j, i, c, row, :]
                out_ref[c, out_row, :] = colour

    def step(s):
        for lag, stage in enumerate((produce, ratios, pair_sums, slab, finish)):
            @pl.when(jnp.logical_and(s >= lag, s < chunks + lag))
            def _():
                stage(s - lag)
    landed(vol.at[0], vol_sem.at[0])
    each(early, lambda off: march(0, (me + 1 + off) % members))
    pl.semaphore_wait(barrier, members + groups - 2)
    each(chunks + 4, step)

    landed(tloc.at[:, pl.ds(0, members - 1)], t_send)
    landed(pcol, c_send)
    landed(mout.at[:, pl.ds(0, chips - 1)], m_send)
    landed(sout.at[:, pl.ds(0, chips - 1)], s_send)
    landed(zout.at[:, pl.ds(0, groups - 1)], z_send)


def solution(mesh):
    groups, members = mesh.shape["grp"], mesh.shape["mem"]
    chips = members // 2

    def body(volume, transfer_coef, group_order, member_order, active_mask):
        samples, image_rows, cols = volume.shape[2:]
        block_rows = image_rows // members
        chunks = min(CHUNKS, block_rows // TILE_ROWS)
        rows = block_rows // chunks
        group_cols = cols // groups
        smem = pl.BlockSpec(memory_space=pltpu.SMEM)
        f32 = jnp.float32
        dma = pltpu.SemaphoreType.DMA
        scratch = [
            pltpu.VMEM((chunks, members, samples, rows, cols), f32),
            pltpu.VMEM((chunks, members, rows, cols), f32),
            pltpu.VMEM((chunks, members, rows, cols), f32),
            pltpu.VMEM((chunks, members, 3, rows, cols), f32),
            pltpu.VMEM((chunks, chips, 3, rows, cols), f32),
            pltpu.VMEM((chunks, chips, rows, cols), f32),
            pltpu.VMEM((chunks, chips, rows, cols), f32),
            pltpu.VMEM((chunks, chips, rows, cols), f32),
            pltpu.VMEM((chunks, rows, cols), f32),
            pltpu.VMEM((chunks, chips, 3, rows, cols), f32),
            pltpu.VMEM((chunks, chips, 3, rows, cols), f32),
            pltpu.VMEM((chunks, groups, 4, rows, group_cols), f32),
            pltpu.VMEM((chunks, groups, 4, rows, group_cols), f32),
            dma((chunks,)),
            dma, dma((chunks,)),
            dma, dma((chunks,)),
            dma, dma((chunks,)),
            dma, dma((chunks,)),
            dma, dma((chunks,)),
        ]
        return pl.pallas_call(
            functools.partial(kernel, groups, members),
            out_shape=jax.ShapeDtypeStruct((4, block_rows, group_cols), f32),
            in_specs=[smem, smem, smem, smem, pl.BlockSpec(memory_space=pl.ANY)],
            out_specs=pl.BlockSpec(memory_space=pltpu.VMEM),
            scratch_shapes=scratch,
            compiler_params=pltpu.CompilerParams(
                collective_id=0, has_side_effects=True, vmem_limit_bytes=60 * 1024 * 1024),
        )(transfer_coef, group_order, member_order, active_mask, volume)

    in_specs = (P("grp", "mem", None, None, None), P(), P(), P(), P("grp", "mem"))
    out_specs = P(None, "mem", "grp")
    return jax.shard_map(body, mesh=mesh, in_specs=in_specs, out_specs=out_specs, check_vma=False)
```

profile of v0, /device:TPU:0, one launch (start us, length us, event | category | flops | bytes accessed | tf_op | source)
XLA Modules:
  0.0 86.1 jit_solution(14012022304509471184)
XLA Ops:
  0.7 83.8 %shard_map.55 = f32[4,64,256]{2,1,0:T(8,128)} custom-call(f32[4,4]{1,0:T(4,128)} %coef_ref.1, s32[4]{0:T(128)} %group_ref.1, s32[4,8]{1,0:T(4,128)} %member_ref.1, s32[1,1]{1,0:T(1,128)S(6)} %copy.7.active_ref, f32[1,1,8,512,1024]{4,3,2,1,0:T(8,128)} %volume_ref.1), custom_call_target="tpu_custom_call" | custom-call | tf_op jit(solution)/shard_map/pallas_call | solution.py:297
  84.4 1.7 %copy.8 = f32[4,64,256]{2,1,0:T(8,128)} copy(f32[4,64,256]{2,1,0:T(8,128)} %shard_map.55) | data formatting | bytes 524288
where the time goes:
time: 86.3 us; the launch traced here: 86.1 us
  Pallas kernels  83.8 us (97%)
  local copies, waits for them, and re-layouts  1.67 us (2%)
    pallas_call x1, Pallas kernels, body(): pl.pallas_call(functools.partial(kernel, groups, members), out_shape=jax....  83.8 us

commit v1 on v0

--- a/solution.py
+++ b/solution.py
@@ -296,7 +296,7 @@
         ]
         return pl.pallas_call(
             functools.partial(kernel, groups, members),
-            out_shape=jax.ShapeDtypeStruct((4, block_rows, group_cols), f32),
+            out_shape=pltpu.VMEM((4, block_rows, group_cols), f32),
             in_specs=[smem, smem, smem, smem, pl.BlockSpec(memory_space=pl.ANY)],
             out_specs=pl.BlockSpec(memory_space=pltpu.VMEM),
             scratch_shapes=scratch,

time: 86.3 us -> 84.6 us (0.980)
  local copies, waits for them, and re-layouts: 1.67 us -> 0.71 us
    unnamed x1, local copies, waits for them, and re-layouts: 1.67 us -> 0.71 us
where the time goes in v1:
time: 84.6 us; the launch traced here: 84.4 us
  Pallas kernels  83.1 us (98%)
    pallas_call x1, Pallas kernels, body(): pl.pallas_call(functools.partial(kernel, groups, members), out_shape=pltp...  83.1 us

profile of v1, /device:TPU:0, one launch (start us, length us, event | category | flops | bytes accessed | tf_op | source)
XLA Modules:
  0.0 84.4 jit_solution(18161313990511788855)
XLA Ops:
  0.7 83.1 %shard_map.55 = f32[4,64,256]{2,1,0:T(8,128)S(1)} custom-call(f32[4,4]{1,0:T(4,128)} %coef_ref.1, s32[4]{0:T(128)} %group_ref.1, s32[4,8]{1,0:T(4,128)} %member_ref.1, s32[1,1]{1,0:T(1,128)S(6)} %copy.8.active_ref, f32[1,1,8,512,1024]{4,3,2,1,0:T(8,128)} %volume_ref.1), custom_call_target="tpu_custom_call" | custom-call | tf_op jit(solution)/shard_map/pallas_call | solution.py:297
  83.7 0.7 copy.7

commit v2 on v1

v2 whole, which is shorter than its diff:
```python
import functools
import math

import jax
import jax.numpy as jnp
from jax import lax
from jax.experimental import pallas as pl
from jax.experimental.pallas import tpu as pltpu
from jax.sharding import PartitionSpec as P

MESH = pl.DeviceIdType.MESH
TILE_ROWS = 8
LANES = 128
HALVES = 2
EARLY = 2
LAGS = (0, 6, 7, 8, 9, 10)


def kernel(groups, members, coef_ref, group_ref, member_ref, active_ref, volume_ref, out_ref,
           vol, tloc, tin, col, pcol, rout, rin, qout, qin, tfirst, tslab, aout, ain, own, bout, bin_,
           zout, zin, vol_sem, t_send, t_recv, c_send, c_recv, r_send, r_recv, q_send, q_recv,
           a_send, a_recv, b_send, b_recv, z_send, z_recv):
    chunks, _, rows, cols = tloc.shape
    stripes, _, samples, _, _ = vol.shape
    block_rows = stripes * rows
    halves = chunks // stripes
    part = cols // groups
    group_cols = part * halves
    chips = members // 2
    pairs = chips // 2
    g = lax.axis_index("grp")
    me = lax.axis_index("mem")
    chip = me // 2
    core = me % 2
    partner = me + 1 - 2 * core

    side = (1 - core) * ((chip // 2) % 2) + core * (chip % 2)
    mate = chip + (1 - core) * (2 - 4 * ((chip // 2) % 2)) + core * (1 - 2 * (chip % 2))
    my_pair = (1 - core) * ((chip // 4) * 2 + chip % 2) + core * (chip // 2)

    def member_of_pair(p, which):
        return (1 - core) * ((p // 2) * 4 + 2 * which + p % 2) + core * (2 * p + which)

    def fetch(j, d):
        start = pl.multiple_of(d * block_rows + j * rows, TILE_ROWS)
        return pltpu.make_async_copy(
            volume_ref.at[0, 0, :, pl.ds(start, rows), :], vol.at[j, d], vol_sem.at[j])

    def send(src, dst, send_sem, recv_sem, device):
        pltpu.make_async_remote_copy(
            src, dst, send_sem, recv_sem, device_id=device, device_id_type=MESH).start()

    def landed(ref, sem):
        pltpu.make_async_copy(ref, ref, sem).wait()

    def each(count, fn):
        def step(i, carry):
            fn(i)
            return carry
        lax.fori_loop(0, count, step, 0)

    each(stripes, lambda j: each(members, lambda off: fetch(j, (me + 1 + off) % members).start()))

    barrier = pltpu.get_barrier_semaphore()
    each(members - 1, lambda off: pl.semaphore_signal(
        barrier, inc=1, device_id={"mem": (me + 1 + off) % members}, device_id_type=MESH))
    each(groups - 1, lambda off: pl.semaphore_signal(
        barrier, inc=1, device_id={"grp": (g + 1 + off) % groups}, device_id_type=MESH))

    density_factor = math.sqrt(3.0 / (samples * groups * members) * math.log2(math.e))
    coef = [[coef_ref[c, p] * (0.5 if c < 3 else density_factor) for p in range(4)] for c in range(4)]
    active = active_ref[0, 0].astype(jnp.float32)
    half_active = active * 0.5
    width = min(512, cols)
    piece = min(part, width)
    ranks = [member_ref[g, i] for i in range(members)]
    near = [jnp.minimum(ranks[2 * q], ranks[2 * q + 1]) for q in range(chips)]
    far = [jnp.maximum(ranks[2 * q], ranks[2 * q + 1]) for q in range(chips)]
    orders = [group_ref[i] for i in range(groups)]

    def rank_of(member):
        return member_ref[g, member]

    def chip_rank(q):
        return jnp.minimum(rank_of(2 * q), rank_of(2 * q + 1))

    own_first = rank_of(me) < rank_of(partner)
    chip_first = chip_rank(chip) < chip_rank(mate)

    def tiles(fn):
        def step(i):
            fn(pl.ds(pl.multiple_of(i * width, width), width))
        if cols == width:
            fn(slice(None))
        else:
            each(cols // width, step)

    def march(i, d):
        j, h = i // halves, i % halves

        def tile(t):
            depth = jnp.zeros((TILE_ROWS, width), jnp.float32)
            light = jnp.ones((TILE_ROWS, width), jnp.float32)
            colour = [jnp.zeros((TILE_ROWS, width), jnp.float32) for _ in range(3)]
            starts = []
            for u in range(width // piece):
                at = t * width + u * piece
                starts.append(pl.multiple_of((at // part) * group_cols + h * part + at % part, LANES))
            column = pl.ds(pl.multiple_of(t * width, LANES), width)
            for k in range(samples):
                v = jnp.concatenate([vol[j, d, k, :, pl.ds(s, piece)] for s in starts], axis=1)
                poly = [q[0] + v * (q[1] + v * (q[2] + v * q[3])) for q in coef]
                depth = depth - poly[3] * poly[3]
                after = jnp.exp2(depth)
                weight = light - after
                light = after
                colour = [colour[c] + weight * jnp.tanh(poly[c]) for c in range(3)]
            coverage = 1.0 - light
            tloc[i, d, :, column] = 1.0 - active * coverage
            for c in range(3):
                col[i, d, c, :, column] = half_active * (coverage + colour[c])
        if cols == width:
            tile(0)
        else:
            each(cols // width, tile)

    early = min(EARLY, chunks)

    def wait_volume(i):
        @pl.when(i % halves == 0)
        def _():
            landed(vol.at[i // halves], vol_sem.at[i // halves])

    def produce(i):
        @pl.when(i >= early)
        def _():
            wait_volume(i)

        def unit(off):
            d = (me + 1 + off) % members

            @pl.when(i >= early)
            def _():
                march(i, d)

            @pl.when(off < members - 1)
            def _():
                send(tloc.at[i, d], tin.at[i, me], t_send, t_recv.at[i], {"mem": d})

            @pl.when(d % 2 != core)
            def _():
                send(col.at[i, d], pcol.at[i, d // 2], c_send, c_recv.at[i], {"mem": partner})
        each(members, unit)
        tin[i, me] = tloc[i, me]

    def ratios(i):
        landed(tin.at[i, pl.ds(0, members - 1)], t_recv.at[i])

        def tile(column):
            t = [tin[i, m, :, column] for m in range(members)]
            one = jnp.ones((TILE_ROWS, width), jnp.float32)
            total = t[0]
            for m in range(1, members):
                total = total * t[m]
            tslab[i, :, column] = total

            def between(low, high):
                product = one
                for m in range(members):
                    inside = ranks[m] < high
                    if low is not None:
                        inside = jnp.logical_and(ranks[m] >= low, inside)
                    product = product * jnp.where(inside, t[m], 1.0)
                return product

            for q in range(chips):
                rout[i, q, :, column] = between(near[q], far[q])
            for p in range(pairs):
                a, b = chip_rank(member_of_pair(p, 0)), chip_rank(member_of_pair(p, 1))
                first, second = jnp.minimum(a, b), jnp.maximum(a, b)
                tfirst[i, p, :, column] = between(None, first)
                qout[i, p, :, column] = between(first, second)
        tiles(tile)

        def to_chip(off):
            k = (chip + 1 + off) % chips
            send(rout.at[i, k], rin.at[i, chip], r_send, r_recv.at[i], {"mem": 2 * k + core})
        each(chips - 1, to_chip)

        def to_pair(off):
            p = (my_pair + 1 + off) % pairs
            send(qout.at[i, p], qin.at[i, my_pair], q_send, q_recv.at[i],
                 {"mem": 2 * member_of_pair(p, side) + core})
        each(pairs - 1, to_pair)
        rin[i, chip] = rout[i, chip]
        qin[i, my_pair] = qout[i, my_pair]

    def chip_sums(i):
        landed(rin.at[i, pl.ds(0, chips - 1)], r_recv.at[i])
        landed(pcol.at[i], c_recv.at[i])

        def sums(k, ref, p):
            def tile(column):
                ratio = rin[i, k, :, column]
                own_factor = jnp.where(own_first, 1.0, ratio)
                other_factor = jnp.where(own_first, ratio, 1.0)
                for c in range(3):
                    ref[i, p, c, :, column] = (
                        col[i, 2 * k + core, c, :, column] * own_factor
                        + pcol[i, k, c, :, column] * other_factor)
            tiles(tile)
        each(pairs, lambda p: sums(member_of_pair(p, 1 - side), aout, p))
        send(aout.at[i], ain.at[i], a_send, a_recv.at[i], {"mem": 2 * mate + core})
        each(pairs, lambda p: sums(member_of_pair(p, side), own, p))

    def pair_sums(i):
        landed(ain.at[i], a_recv.at[i])
        if pairs > 1:
            landed(qin.at[i, pl.ds(0, pairs - 1)], q_recv.at[i])

        def unit(off):
            p = (my_pair + 1 + off) % pairs

            def tile(column):
                ratio = qin[i, p, :, column]
                own_factor = jnp.where(chip_first, 1.0, ratio)
                other_factor = jnp.where(chip_first, ratio, 1.0)
                for c in range(3):
                    bout[i, p, c, :, column] = (
                        own[i, p, c, :, column] * own_factor + ain[i, p, c, :, column] * other_factor)
            tiles(tile)

            @pl.when(off < pairs - 1)
            def _():
                send(bout.at[i, p], bin_.at[i, my_pair], b_send, b_recv.at[i],
                     {"mem": 2 * member_of_pair(p, side) + core})
        each(pairs, unit)
        bin_[i, my_pair] = bout[i, my_pair]

    def slab(i):
        if pairs > 1:
            landed(bin_.at[i, pl.ds(0, pairs - 1)], b_recv.at[i])
        for k in range(groups):
            column = pl.ds(k * part, part)
            factor = [tfirst[i, p, :, column] for p in range(pairs)]
            for c in range(3):
                total = factor[0] * bin_[i, 0, c, :, column]
                for p in range(1, pairs):
                    total = total + factor[p] * bin_[i, p, c, :, column]
                zout[i, k, c] = total
            zout[i, k, 3] = tslab[i, :, column]

        def unit(off):
            k = (g + 1 + off) % groups
            send(zout.at[i, k], zin.at[i, g], z_send, z_recv.at[i], {"grp": k})
        each(groups - 1, unit)
        zin[i, g] = zout[i, g]

    def finish(i):
        landed(zin.at[i, pl.ds(0, groups - 1)], z_recv.at[i])
        row = pl.ds(pl.multiple_of((i // halves) * TILE_ROWS, TILE_ROWS), TILE_ROWS)
        column = pl.ds(pl.multiple_of((i % halves) * part, LANES), part)
        t = [zin[i, k, 3] for k in range(groups)]
        total = t[0]
        for k in range(1, groups):
            total = total * t[k]
        out_ref[3, row, column] = 1.0 - total
        factor = []
        for k in range(groups):
            before = jnp.ones_like(total)
            for o in range(groups):
                if o != k:
                    before = before * jnp.where(orders[o] < orders[k], t[o], 1.0)
            factor.append(before)
        for c in range(3):
            colour = factor[0] * zin[i, 0, c]
            for k in range(1, groups):
                colour = colour + factor[k] * zin[i, k, c]
            out_ref[c, row, column] = colour

    stages = (produce, ratios, chip_sums, pair_sums, slab, finish)

    def step(s):
        for lag, stage in zip(LAGS, stages):
            @pl.when(jnp.logical_and(s >= lag, s < chunks + lag))
            def _():
                stage(s - lag)

    def first(i):
        wait_volume(i)
        each(members, lambda off: march(i, (me + 1 + off) % members))
    each(early, first)
    pl.semaphore_wait(barrier, members + groups - 2)
    each(chunks + LAGS[-1], step)

    landed(tloc.at[:, pl.ds(0, members - 1)], t_send)
    landed(pcol, c_send)
    landed(rout.at[:, pl.ds(0, chips - 1)], r_send)
    if pairs > 1:
        landed(qout.at[:, pl.ds(0, pairs - 1)], q_send)
        landed(bout.at[:, pl.ds(0, pairs - 1)], b_send)
    landed(aout, a_send)
    landed(zout.at[:, pl.ds(0, groups - 1)], z_send)


def solution(mesh):
    groups, members = mesh.shape["grp"], mesh.shape["mem"]
    chips = members // 2
    pairs = chips // 2

    def body(volume, transfer_coef, group_order, member_order, active_mask):
        samples, image_rows, cols = volume.shape[2:]
        block_rows = image_rows // members
        stripes = block_rows // TILE_ROWS
        group_cols = cols // groups
        halves = min(HALVES, group_cols // LANES)
        part = group_cols // halves
        wide = part * groups
        chunks = stripes * halves
        smem = pl.BlockSpec(memory_space=pltpu.SMEM)
        dma = pltpu.SemaphoreType.DMA

        def vmem(*shape):
            return pltpu.VMEM(shape, jnp.float32)

        tile = (TILE_ROWS, wide)
        scratch = [
            vmem(stripes, members, samples, TILE_ROWS, cols),
            vmem(chunks, members, *tile),
            vmem(chunks, members, *tile),
            vmem(chunks, members, 3, *tile),
            vmem(chunks, chips, 3, *tile),
            vmem(chunks, chips, *tile),
            vmem(chunks, chips, *tile),
            vmem(chunks, pairs, *tile),
            vmem(chunks, pairs, *tile),
            vmem(chunks, pairs, *tile),
            vmem(chunks, *tile),
            vmem(chunks, pairs, 3, *tile),
            vmem(chunks, pairs, 3, *tile),
            vmem(chunks, pairs, 3, *tile),
            vmem(chunks, pairs, 3, *tile),
            vmem(chunks, pairs, 3, *tile),
            vmem(chunks, groups, 4, TILE_ROWS, part),
            vmem(chunks, groups, 4, TILE_ROWS, part),
            dma((stripes,)),
        ]
        for _ in range(7):
            scratch += [dma, dma((chunks,))]
        return pl.pallas_call(
            functools.partial(kernel, groups, members),
            out_shape=pltpu.VMEM((4, block_rows, group_cols), jnp.float32),
            in_specs=[smem, smem, smem, smem, pl.BlockSpec(memory_space=pl.ANY)],
            out_specs=pl.BlockSpec(memory_space=pltpu.VMEM),
            scratch_shapes=scratch,
            compiler_params=pltpu.CompilerParams(
                collective_id=0, has_side_effects=True, vmem_limit_bytes=60 * 1024 * 1024),
        )(transfer_coef, group_order, member_order, active_mask, volume)

    in_specs = (P("grp", "mem", None, None, None), P(), P(), P(), P("grp", "mem"))
    out_specs = P(None, "mem", "grp")
    return jax.shard_map(body, mesh=mesh, in_specs=in_specs, out_specs=out_specs, check_vma=False)
```

time: 84.6 us -> 89.2 us (1.054)
  Pallas kernels: 83.1 us -> 87.6 us
    pallas_call x1, Pallas kernels: 83.1 us -> 87.6 us  [body(): pl.pallas_call(functools.partial(kernel, groups, members), out_shape=pltp...]
where the time goes in v2:
time: 89.2 us; the launch traced here: 89 us
  Pallas kernels  87.6 us (98%)
    pallas_call x1, Pallas kernels, body(): pl.pallas_call(functools.partial(kernel, groups, members), out_shape=pltp...  87.6 us

profile of v2, /device:TPU:0, one launch (start us, length us, event | category | flops | bytes accessed | tf_op | source)
XLA Modules:
  0.0 89.0 jit_solution(7154427065281225079)
XLA Ops:
  0.7 87.6 %shard_map.55 = f32[4,64,256]{2,1,0:T(8,128)S(1)} custom-call(f32[4,4]{1,0:T(4,128)} %coef_ref.1, s32[4]{0:T(128)} %group_ref.1, s32[4,8]{1,0:T(4,128)} %member_ref.1, s32[1,1]{1,0:T(1,128)S(6)} %copy.8.active_ref, f32[1,1,8,512,1024]{4,3,2,1,0:T(8,128)} %volume_ref.1), custom_call_target="tpu_custom_call" | custom-call | tf_op jit(solution)/shard_map/pallas_call | solution.py:350
  88.3 0.7 copy.7

commit v3 on v2

v3 whole, which is shorter than its diff:
```python
import functools
import math

import jax
import jax.numpy as jnp
from jax import lax
from jax.experimental import pallas as pl
from jax.experimental.pallas import tpu as pltpu
from jax.sharding import PartitionSpec as P

MESH = pl.DeviceIdType.MESH
TILE_ROWS = 8
LANES = 128
HALVES = 2
EARLY = 3
LAGS = (0, 2, 4, 4, 6, 8, 10)


def kernel(groups, members, coef_ref, group_ref, member_ref, active_ref, volume_ref, out_ref,
           vol, tloc, tin, col, rout, qout, inbox, aout, ain, own, fout, fin, tout, tpin, zout, zin,
           yout, yin, vol_sem, t_send, t_recv, c_send, r_send, q_send, m_recv, p_send, p_recv,
           a_send, a_recv, f_send, z_send, z_recv, y_send, y_recv):
    chunks, _, rows, width = tloc.shape
    stripes, samples, _, _, _ = vol.shape
    halves = chunks // stripes
    part = width // groups
    group_cols = part * halves
    chips = members // 2
    pairs = chips // 2
    g = lax.axis_index("grp")
    me = lax.axis_index("mem")
    chip = me // 2
    core = me % 2
    partner = me + 1 - 2 * core

    def bit(i):
        return (core + i) % 2

    def side(i):
        return (1 - bit(i)) * ((chip // 2) % 2) + bit(i) * (chip % 2)

    def mate(i):
        return chip + (1 - bit(i)) * (2 - 4 * ((chip // 2) % 2)) + bit(i) * (1 - 2 * (chip % 2))

    def pair_of(i):
        return (1 - bit(i)) * ((chip // 4) * 2 + chip % 2) + bit(i) * (chip // 2)

    def chip_of_pair(i, p, which):
        return (1 - bit(i)) * ((p // 2) * 4 + 2 * which + p % 2) + bit(i) * (2 * p + which)

    from_chip, from_pair = 3 * chips, 4 * chips
    sums_of_group = 3 * pairs
    factors_at = (groups - 1) * sums_of_group

    def fetch_first(d):
        return pltpu.make_async_copy(
            volume_ref.at[:, d, pl.ds(0, rows), :], vol.at[0, :, d], vol_sem.at[d])

    def fetch(j):
        start = pl.multiple_of(j * rows, TILE_ROWS)
        return pltpu.make_async_copy(
            volume_ref.at[:, :, pl.ds(start, rows), :], vol.at[j], vol_sem.at[members - 1 + j])

    def send(src, dst, send_sem, recv_sem, device):
        pltpu.make_async_remote_copy(
            src, dst, send_sem, recv_sem, device_id=device, device_id_type=MESH).start()

    def landed(ref, sem):
        pltpu.make_async_copy(ref, ref, sem).wait()

    def each(count, fn):
        def step(i, carry):
            fn(i)
            return carry
        lax.fori_loop(0, count, step, 0)

    barrier = pltpu.get_barrier_semaphore()
    each(members - 1, lambda off: pl.semaphore_signal(
        barrier, inc=1, device_id={"mem": (me + 1 + off) % members}, device_id_type=MESH))
    each(groups - 1, lambda off: pl.semaphore_signal(
        barrier, inc=1, device_id={"grp": (g + 1 + off) % groups}, device_id_type=MESH))

    each(members, lambda off: fetch_first((me + 1 + off) % members).start())
    each(stripes - 1, lambda j: fetch(j + 1).start())

    density_factor = math.sqrt(3.0 / (samples * groups * members) * math.log2(math.e))
    coef = [[coef_ref[c, p] * (0.5 if c < 3 else density_factor) for p in range(4)] for c in range(4)]
    active = active_ref[0, 0].astype(jnp.float32)
    half_active = active * 0.5
    ranks = [member_ref[g, i] for i in range(members)]
    near = [jnp.minimum(ranks[2 * q], ranks[2 * q + 1]) for q in range(chips)]
    far = [jnp.maximum(ranks[2 * q], ranks[2 * q + 1]) for q in range(chips)]
    orders = [group_ref[(g + groups - 1 - e) % groups] for e in range(groups)]

    def rank_of(member):
        return member_ref[g, member]

    def chip_rank(q):
        return jnp.minimum(rank_of(2 * q), rank_of(2 * q + 1))

    own_first = rank_of(me) < rank_of(partner)

    def march(i, d):
        j, h = i // halves, i % halves
        depth = jnp.zeros((TILE_ROWS, width), jnp.float32)
        light = jnp.ones((TILE_ROWS, width), jnp.float32)
        colour = [jnp.zeros((TILE_ROWS, width), jnp.float32) for _ in range(3)]
        starts = [pl.multiple_of(k * group_cols + h * part, LANES) for k in range(groups)]
        for k in range(samples):
            v = jnp.concatenate([vol[j, k, d, :, pl.ds(s, part)] for s in starts], axis=1)
            poly = [q[0] + v * (q[1] + v * (q[2] + v * q[3])) for q in coef]
            depth = depth - poly[3] * poly[3]
            after = jnp.exp2(depth)
            weight = light - after
            light = after
            colour = [colour[c] + weight * jnp.tanh(poly[c]) for c in range(3)]
        coverage = 1.0 - light
        tloc[i, d] = 1.0 - active * coverage
        for c in range(3):
            col[i, d, c] = half_active * (coverage + colour[c])

    early = min(EARLY, members)

    def prepare(i, off):
        d = (me + 1 + off) % members

        @pl.when(i == 0)
        def _():
            fetch_first(d).wait()
        march(i, d)

    def produce(i):
        @pl.when(jnp.logical_and(i > 0, i % halves == 0))
        def _():
            fetch(i // halves).wait()

        def unit(off):
            d = (me + 1 + off) % members

            @pl.when(jnp.logical_or(i > 0, off >= early))
            def _():
                prepare(i, off)

            @pl.when(off < members - 1)
            def _():
                send(tloc.at[i, d], tin.at[i, me], t_send, t_recv.at[i], {"mem": d})

            @pl.when(d % 2 != core)
            def _():
                send(col.at[i, d], inbox.at[i, pl.ds(3 * (d // 2), 3)], c_send, m_recv.at[i],
                     {"mem": partner})
        each(members, unit)
        tin[i, me] = tloc[i, me]

    def ratios(i):
        landed(tin.at[i, pl.ds(0, members - 1)], t_recv.at[i])
        t = [tin[i, m] for m in range(members)]

        def between(low, high):
            product = jnp.ones((TILE_ROWS, width), jnp.float32)
            for m in range(members):
                inside = ranks[m] < high
                if low is not None:
                    inside = jnp.logical_and(ranks[m] >= low, inside)
                product = product * jnp.where(inside, t[m], 1.0)
            return product

        def by_group(at, value):
            for k in range(groups):
                tout[i, k, at] = value[:, k * part:(k + 1) * part]

        for q in range(chips):
            rout[i, q] = between(near[q], far[q])

        def to_chip(off):
            k = (chip + 1 + off) % chips
            send(rout.at[i, k], inbox.at[i, from_chip + off], r_send, m_recv.at[i], {"mem": 2 * k + core})
        each(chips - 1, to_chip)

        total = t[0]
        for m in range(1, members):
            total = total * t[m]
        by_group(0, total)
        for p in range(pairs):
            a, b = chip_rank(chip_of_pair(i, p, 0)), chip_rank(chip_of_pair(i, p, 1))
            first, second = jnp.minimum(a, b), jnp.maximum(a, b)
            by_group(1 + p, between(None, first))
            qout[i, p] = between(first, second)
        my_pair = pair_of(i)

        def to_pair(off):
            p = (my_pair + 1 + off) % pairs
            send(qout.at[i, p], inbox.at[i, from_pair + off], q_send, m_recv.at[i],
                 {"mem": 2 * chip_of_pair(i, p, side(i)) + core})
        each(pairs - 1, to_pair)

        def to_group(off):
            k = (g + 1 + off) % groups
            send(tout.at[i, k], tpin.at[i, off], p_send, p_recv.at[i], {"grp": k})
        each(groups - 1, to_group)
        inbox[i, from_chip + chips - 1] = rout[i, chip]
        inbox[i, from_pair + pairs - 1] = qout[i, my_pair]
        tpin[i, groups - 1] = tout[i, g]

    def factors(i):
        landed(tpin.at[i, pl.ds(0, groups - 1)], p_recv.at[i])
        t = [tpin[i, e, 0] for e in range(groups)]
        total = t[0]
        for e in range(1, groups):
            total = total * t[e]
        row = pl.ds(pl.multiple_of((i // halves) * TILE_ROWS, TILE_ROWS), TILE_ROWS)
        column = pl.ds(pl.multiple_of((i % halves) * part, LANES), part)
        out_ref[3, row, column] = 1.0 - total
        for e in range(groups):
            before = jnp.ones_like(total)
            for o in range(groups):
                if o != e:
                    before = before * jnp.where(orders[o] < orders[e], t[o], 1.0)
            for p in range(pairs):
                fout[i, p, e] = before * tpin[i, e, 1 + p]
        my_pair = pair_of(i)

        def to_pair(off):
            p = (my_pair + 1 + off) % pairs
            send(fout.at[i, p], zin.at[i, pl.ds(factors_at + off * groups, groups)], f_send, z_recv.at[i],
                 {"mem": 2 * chip_of_pair(i, p, side(i)) + core})
        each(pairs - 1, to_pair)
        fin[i] = fout[i, my_pair]

    def chip_sums(i):
        landed(inbox.at[i, pl.ds(0, 4 * chips + pairs - 2)], m_recv.at[i])

        def sums(k, ref, p):
            ratio = inbox[i, from_chip + (chip - k - 1 + chips) % chips]
            own_factor = jnp.where(own_first, 1.0, ratio)
            other_factor = jnp.where(own_first, ratio, 1.0)
            for c in range(3):
                ref[i, p, c] = col[i, 2 * k + core, c] * own_factor + inbox[i, 3 * k + c] * other_factor
        each(pairs, lambda p: sums(chip_of_pair(i, p, 1 - side(i)), aout, p))
        send(aout.at[i], ain.at[i], a_send, a_recv.at[i], {"mem": 2 * mate(i) + core})
        each(pairs, lambda p: sums(chip_of_pair(i, p, side(i)), own, p))

    def pair_sums(i):
        landed(ain.at[i], a_recv.at[i])
        my_pair = pair_of(i)
        chip_first = chip_rank(chip) < chip_rank(mate(i))

        def unit(p):
            ratio = inbox[i, from_pair + (my_pair - p - 1 + pairs) % pairs]
            own_factor = jnp.where(chip_first, 1.0, ratio)
            other_factor = jnp.where(chip_first, ratio, 1.0)
            for c in range(3):
                total = own[i, p, c] * own_factor + ain[i, p, c] * other_factor
                for k in range(groups):
                    zout[i, k, 3 * p + c] = total[:, k * part:(k + 1) * part]
        each(pairs, unit)

        def to_group(off):
            k = (g + 1 + off) % groups
            send(zout.at[i, k], zin.at[i, pl.ds(off * sums_of_group, sums_of_group)], z_send, z_recv.at[i],
                 {"grp": k})
        each(groups - 1, to_group)

    def combine(i):
        landed(zin.at[i, pl.ds(0, factors_at + (pairs - 1) * groups)], z_recv.at[i])
        my_pair = pair_of(i)

        def sums(p, factor, ref, at):
            for c in range(3):
                total = factor(groups - 1) * zout[i, g, 3 * p + c]
                for e in range(groups - 1):
                    total = total + factor(e) * zin[i, e * sums_of_group + 3 * p + c]
                ref[i, at, c] = total

        def unit(off):
            p = (my_pair + 1 + off) % pairs
            back = (my_pair - p - 1 + pairs) % pairs
            sums(p, lambda e: zin[i, factors_at + back * groups + e], yout, p)
            send(yout.at[i, p], yin.at[i, off], y_send, y_recv.at[i],
                 {"mem": 2 * chip_of_pair(i, p, side(i)) + core})
        each(pairs - 1, unit)
        sums(my_pair, lambda e: fin[i, e], yin, pairs - 1)

    def finish(i):
        if pairs > 1:
            landed(yin.at[i, pl.ds(0, pairs - 1)], y_recv.at[i])
        row = pl.ds(pl.multiple_of((i // halves) * TILE_ROWS, TILE_ROWS), TILE_ROWS)
        column = pl.ds(pl.multiple_of((i % halves) * part, LANES), part)
        for c in range(3):
            colour = yin[i, 0, c]
            for p in range(1, pairs):
                colour = colour + yin[i, p, c]
            out_ref[c, row, column] = colour

    stages = (produce, ratios, factors, chip_sums, pair_sums, combine, finish)

    def step(s):
        for lag, stage in zip(LAGS, stages):
            @pl.when(jnp.logical_and(s >= lag, s < chunks + lag))
            def _():
                stage(s - lag)

    each(early, lambda off: prepare(0, off))
    pl.semaphore_wait(barrier, members + groups - 2)
    each(chunks + LAGS[-1], step)

    landed(tloc.at[:, pl.ds(0, members - 1)], t_send)
    landed(inbox.at[:, pl.ds(0, 3 * chips)], c_send)
    landed(rout.at[:, pl.ds(0, chips - 1)], r_send)
    landed(tout.at[:, pl.ds(0, groups - 1)], p_send)
    landed(aout, a_send)
    landed(zout.at[:, pl.ds(0, groups - 1)], z_send)
    if pairs > 1:
        landed(qout.at[:, pl.ds(0, pairs - 1)], q_send)
        landed(fout.at[:, pl.ds(0, pairs - 1)], f_send)
        landed(yout.at[:, pl.ds(0, pairs - 1)], y_send)


def solution(mesh):
    groups, members = mesh.shape["grp"], mesh.shape["mem"]
    chips = members // 2
    pairs = chips // 2

    def body(volume, transfer_coef, group_order, member_order, active_mask):
        samples, image_rows, cols = volume.shape[2:]
        block_rows = image_rows // members
        stripes = block_rows // TILE_ROWS
        group_cols = cols // groups
        halves = min(HALVES, group_cols // LANES)
        part = group_cols // halves
        chunks = stripes * halves
        smem = pl.BlockSpec(memory_space=pltpu.SMEM)
        dma = pltpu.SemaphoreType.DMA

        def vmem(*shape):
            return pltpu.VMEM(shape, jnp.float32)

        tile = (TILE_ROWS, part * groups)
        piece = (TILE_ROWS, part)
        scratch = [
            vmem(stripes, samples, members, TILE_ROWS, cols),
            vmem(chunks, members, *tile),
            vmem(chunks, members, *tile),
            vmem(chunks, members, 3, *tile),
            vmem(chunks, chips, *tile),
            vmem(chunks, pairs, *tile),
            vmem(chunks, 4 * chips + pairs, *tile),
            vmem(chunks, pairs, 3, *tile),
            vmem(chunks, pairs, 3, *tile),
            vmem(chunks, pairs, 3, *tile),
            vmem(chunks, pairs, groups, *piece),
            vmem(chunks, groups, *piece),
            vmem(chunks, groups, 1 + pairs, *piece),
            vmem(chunks, groups, 1 + pairs, *piece),
            vmem(chunks, groups, 3 * pairs, *piece),
            vmem(chunks, (groups - 1) * 3 * pairs + (pairs - 1) * groups, *piece),
            vmem(chunks, pairs, 3, *piece),
            vmem(chunks, pairs, 3, *piece),
            dma((stripes + members - 1,)),
            dma, dma((chunks,)),
            dma, dma, dma, dma((chunks,)),
            dma, dma((chunks,)),
            dma, dma((chunks,)),
            dma, dma, dma((chunks,)),
            dma, dma((chunks,)),
        ]
        return pl.pallas_call(
            functools.partial(kernel, groups, members),
            out_shape=pltpu.VMEM((4, block_rows, group_cols), jnp.float32),
            in_specs=[smem, smem, smem, smem, pl.BlockSpec(memory_space=pl.ANY)],
            out_specs=pl.BlockSpec(memory_space=pltpu.VMEM),
            scratch_shapes=scratch,
            compiler_params=pltpu.CompilerParams(
                collective_id=0, has_side_effects=True, vmem_limit_bytes=60 * 1024 * 1024),
        )(transfer_coef, group_order, member_order, active_mask,
          volume.reshape(samples, members, block_rows, cols))

    in_specs = (P("grp", "mem", None, None, None), P(), P(), P(), P("grp", "mem"))
    out_specs = P(None, "mem", "grp")
    return jax.shard_map(body, mesh=mesh, in_specs=in_specs, out_specs=out_specs, check_vma=False)
```

time: 89.2 us -> 78 us (0.87)
  Pallas kernels: 87.6 us -> 76.4 us
    pallas_call x1, Pallas kernels: 87.6 us -> 76.4 us  [body(): pl.pallas_call(functools.partial(kernel, groups, members), out_shape=pltp...]
where the time goes in v3:
time: 78 us; the launch traced here: 77.8 us
  Pallas kernels  76.4 us (98%)
    pallas_call x1, Pallas kernels, body(): pl.pallas_call(functools.partial(kernel, groups, members), out_shape=pltp...  76.4 us

profile of v3, /device:TPU:0, one launch (start us, length us, event | category | flops | bytes accessed | tf_op | source)
XLA Modules:
  0.0 77.8 jit_solution(132753216126081010)
XLA Ops:
  0.7 76.4 %shard_map.55 = f32[4,64,256]{2,1,0:T(8,128)S(1)} custom-call(f32[4,4]{1,0:T(4,128)} %coef_ref.1, s32[4]{0:T(128)} %group_ref.1, s32[4,8]{1,0:T(4,128)} %member_ref.1, s32[1,1]{1,0:T(1,128)S(6)} %copy.8.active_ref, f32[8,8,64,1024]{3,2,1,0:T(8,128)} %bitcast.1), custom_call_target="tpu_custom_call" | custom-call | tf_op jit(solution)/shard_map/pallas_call | solution.py:367
  77.1 0.7 copy.7

commit v4 on v3

--- a/solution.py
+++ b/solution.py
@@ -13,13 +13,13 @@
 LANES = 128
 HALVES = 2
 EARLY = 3
-LAGS = (0, 2, 4, 4, 6, 8, 10)
+LAGS = (0, 2, 16, 4, 6, 26, 38)
 
 
 def kernel(groups, members, coef_ref, group_ref, member_ref, active_ref, volume_ref, out_ref,
-           vol, tloc, tin, col, rout, qout, inbox, aout, ain, own, fout, fin, tout, tpin, zout, zin,
-           yout, yin, vol_sem, t_send, t_recv, c_send, r_send, q_send, m_recv, p_send, p_recv,
-           a_send, a_recv, f_send, z_send, z_recv, y_send, y_recv):
+           vol, tloc, tin, col, rout, qout, inbox, aout, ain, own, tfirst, fout, fin, tout, tpin, zout, zin,
+           yout, last, vol_sem, t_send, t_recv, c_send, r_send, q_send, m_recv, p_send, p_recv,
+           a_send, f_send, z_send, z_recv, y_send, l_recv):
     chunks, _, rows, width = tloc.shape
     stripes, samples, _, _, _ = vol.shape
     halves = chunks // stripes
@@ -49,8 +49,13 @@
         return (1 - bit(i)) * ((p // 2) * 4 + 2 * which + p % 2) + bit(i) * (2 * p + which)
 
     from_chip, from_pair = 3 * chips, 4 * chips
-    sums_of_group = 3 * pairs
+    sums_of_group = 3 * (pairs - 1)
     factors_at = (groups - 1) * sums_of_group
+    colours_at = (groups - 1) * 3
+    low_half = 1 - g // (groups // 2)
+
+    def far_first(n):
+        return low_half * (groups - 2 - n) + (1 - low_half) * n
 
     def fetch_first(d):
         return pltpu.make_async_copy(
@@ -181,25 +186,31 @@
         for m in range(1, members):
             total = total * t[m]
         by_group(0, total)
-        for p in range(pairs):
+        my_pair = pair_of(i)
+        for off in range(pairs):
+            p = (my_pair + 1 + off) % pairs
             a, b = chip_rank(chip_of_pair(i, p, 0)), chip_rank(chip_of_pair(i, p, 1))
             first, second = jnp.minimum(a, b), jnp.maximum(a, b)
-            by_group(1 + p, between(None, first))
-            qout[i, p] = between(first, second)
-        my_pair = pair_of(i)
+            ahead = between(None, first)
+            if off < pairs - 1:
+                qout[i, off] = between(first, second)
+                by_group(1 + off, ahead)
+            else:
+                inbox[i, from_pair + off] = between(first, second)
+                tfirst[i] = ahead
 
         def to_pair(off):
             p = (my_pair + 1 + off) % pairs
-            send(qout.at[i, p], inbox.at[i, from_pair + off], q_send, m_recv.at[i],
+            send(qout.at[i, off], inbox.at[i, from_pair + off], q_send, m_recv.at[i],
                  {"mem": 2 * chip_of_pair(i, p, side(i)) + core})
         each(pairs - 1, to_pair)
 
-        def to_group(off):
+        def to_group(n):
+            off = far_first(n)
             k = (g + 1 + off) % groups
             send(tout.at[i, k], tpin.at[i, off], p_send, p_recv.at[i], {"grp": k})
         each(groups - 1, to_group)
         inbox[i, from_chip + chips - 1] = rout[i, chip]
-        inbox[i, from_pair + pairs - 1] = qout[i, my_pair]
         tpin[i, groups - 1] = tout[i, g]
 
     def factors(i):
@@ -216,16 +227,16 @@
             for o in range(groups):
                 if o != e:
                     before = before * jnp.where(orders[o] < orders[e], t[o], 1.0)
-            for p in range(pairs):
-                fout[i, p, e] = before * tpin[i, e, 1 + p]
+            fin[i, e] = before
+            for off in range(pairs - 1):
+                fout[i, off, e] = before * tpin[i, e, 1 + off]
         my_pair = pair_of(i)
 
         def to_pair(off):
             p = (my_pair + 1 + off) % pairs
-            send(fout.at[i, p], zin.at[i, pl.ds(factors_at + off * groups, groups)], f_send, z_recv.at[i],
+            send(fout.at[i, off], zin.at[i, pl.ds(factors_at + off * groups, groups)], f_send, z_recv.at[i],
                  {"mem": 2 * chip_of_pair(i, p, side(i)) + core})
         each(pairs - 1, to_pair)
-        fin[i] = fout[i, my_pair]
 
     def chip_sums(i):
         landed(inbox.at[i, pl.ds(0, 4 * chips + pairs - 2)], m_recv.at[i])
@@ -237,59 +248,69 @@
             for c in range(3):
                 ref[i, p, c] = col[i, 2 * k + core, c] * own_factor + inbox[i, 3 * k + c] * other_factor
         each(pairs, lambda p: sums(chip_of_pair(i, p, 1 - side(i)), aout, p))
-        send(aout.at[i], ain.at[i], a_send, a_recv.at[i], {"mem": 2 * mate(i) + core})
+        send(aout.at[i], ain.at[i], a_send, t_recv.at[i], {"mem": 2 * mate(i) + core})
         each(pairs, lambda p: sums(chip_of_pair(i, p, side(i)), own, p))
 
     def pair_sums(i):
-        landed(ain.at[i], a_recv.at[i])
+        landed(ain.at[i], t_recv.at[i])
         my_pair = pair_of(i)
         chip_first = chip_rank(chip) < chip_rank(mate(i))
 
-        def unit(p):
-            ratio = inbox[i, from_pair + (my_pair - p - 1 + pairs) % pairs]
+        def sums(off, scale):
+            p = (my_pair + 1 + off) % pairs
+            ratio = inbox[i, from_pair + (pairs - 2 - off) % pairs]
             own_factor = jnp.where(chip_first, 1.0, ratio)
             other_factor = jnp.where(chip_first, ratio, 1.0)
             for c in range(3):
                 total = own[i, p, c] * own_factor + ain[i, p, c] * other_factor
+                if scale is not None:
+                    total = total * scale
                 for k in range(groups):
-                    zout[i, k, 3 * p + c] = total[:, k * part:(k + 1) * part]
-        each(pairs, unit)
-
-        def to_group(off):
+                    zout[i, k, 3 * off + c] = total[:, k * part:(k + 1) * part]
+
+        for off in range(pairs - 1):
+            sums(off, None)
+
+        def others_to_group(n):
+            off = far_first(n)
             k = (g + 1 + off) % groups
-            send(zout.at[i, k], zin.at[i, pl.ds(off * sums_of_group, sums_of_group)], z_send, z_recv.at[i],
-                 {"grp": k})
-        each(groups - 1, to_group)
+            send(zout.at[i, k, pl.ds(0, sums_of_group)],
+                 zin.at[i, pl.ds(off * sums_of_group, sums_of_group)], z_send, z_recv.at[i], {"grp": k})
+        each(groups - 1, others_to_group)
+        sums(pairs - 1, tfirst[i])
+
+        def own_to_group(n):
+            off = far_first(n)
+            k = (g + 1 + off) % groups
+            send(zout.at[i, k, pl.ds(sums_of_group, 3)], last.at[i, pl.ds(off * 3, 3)],
+                 z_send, l_recv.at[i], {"grp": k})
+        each(groups - 1, own_to_group)
 
     def combine(i):
         landed(zin.at[i, pl.ds(0, factors_at + (pairs - 1) * groups)], z_recv.at[i])
         my_pair = pair_of(i)
 
-        def sums(p, factor, ref, at):
+        for off in range(pairs - 1):
+            p = (my_pair + 1 + off) % pairs
+            back = factors_at + (pairs - 2 - off) * groups
             for c in range(3):
-                total = factor(groups - 1) * zout[i, g, 3 * p + c]
+                total = zin[i, back + groups - 1] * zout[i, g, 3 * off + c]
                 for e in range(groups - 1):
-                    total = total + factor(e) * zin[i, e * sums_of_group + 3 * p + c]
-                ref[i, at, c] = total
-
-        def unit(off):
-            p = (my_pair + 1 + off) % pairs
-            back = (my_pair - p - 1 + pairs) % pairs
-            sums(p, lambda e: zin[i, factors_at + back * groups + e], yout, p)
-            send(yout.at[i, p], yin.at[i, off], y_send, y_recv.at[i],
+                    total = total + zin[i, back + e] * zin[i, e * sums_of_group + 3 * off + c]
+                yout[i, off, c] = total
+            send(yout.at[i, off], last.at[i, pl.ds(colours_at + 3 * off, 3)], y_send, l_recv.at[i],
                  {"mem": 2 * chip_of_pair(i, p, side(i)) + core})
-        each(pairs - 1, unit)
-        sums(my_pair, lambda e: fin[i, e], yin, pairs - 1)
 
     def finish(i):
-        if pairs > 1:
-            landed(yin.at[i, pl.ds(0, pairs - 1)], y_recv.at[i])
+        landed(last.at[i, pl.ds(0, colours_at + sums_of_group)], l_recv.at[i])
         row = pl.ds(pl.multiple_of((i // halves) * TILE_ROWS, TILE_ROWS), TILE_ROWS)
         column = pl.ds(pl.multiple_of((i % halves) * part, LANES), part)
         for c in range(3):
-            colour = yin[i, 0, c]
-            for p in range(1, pairs):
-                colour = colour + yin[i, p, c]
+            colour = fin[i, groups - 1] * zout[i, g, sums_of_group + c]
+            for e in range(groups - 1):
+                colour = colour + fin[i, e] * last[i, e * 3 + c]
+            for off in range(pairs - 1):
+                colour = colour + last[i, colours_at + 3 * off + c]
             out_ref[c, row, column] = colour
 
     stages = (produce, ratios, factors, chip_sums, pair_sums, combine, finish)
@@ -310,10 +331,9 @@
     landed(tout.at[:, pl.ds(0, groups - 1)], p_send)
     landed(aout, a_send)
     landed(zout.at[:, pl.ds(0, groups - 1)], z_send)
-    if pairs > 1:
-        landed(qout.at[:, pl.ds(0, pairs - 1)], q_send)
-        landed(fout.at[:, pl.ds(0, pairs - 1)], f_send)
-        landed(yout.at[:, pl.ds(0, pairs - 1)], y_send)
+    landed(qout, q_send)
+    landed(fout, f_send)
+    landed(yout, y_send)
 
 
 def solution(mesh):
@@ -343,24 +363,25 @@
             vmem(chunks, members, *tile),
             vmem(chunks, members, 3, *tile),
             vmem(chunks, chips, *tile),
-            vmem(chunks, pairs, *tile),
+            vmem(chunks, pairs - 1, *tile),
             vmem(chunks, 4 * chips + pairs, *tile),
             vmem(chunks, pairs, 3, *tile),
             vmem(chunks, pairs, 3, *tile),
             vmem(chunks, pairs, 3, *tile),
-            vmem(chunks, pairs, groups, *piece),
+            vmem(chunks, *tile),
+            vmem(chunks, pairs - 1, groups, *piece),
             vmem(chunks, groups, *piece),
-            vmem(chunks, groups, 1 + pairs, *piece),
-            vmem(chunks, groups, 1 + pairs, *piece),
+            vmem(chunks, groups, pairs, *piece),
+            vmem(chunks, groups, pairs, *piece),
             vmem(chunks, groups, 3 * pairs, *piece),
-            vmem(chunks, (groups - 1) * 3 * pairs + (pairs - 1) * groups, *piece),
-            vmem(chunks, pairs, 3, *piece),
-            vmem(chunks, pairs, 3, *piece),
+            vmem(chunks, (groups - 1) * 3 * (pairs - 1) + (pairs - 1) * groups, *piece),
+            vmem(chunks, pairs - 1, 3, *piece),
+            vmem(chunks, (groups - 1) * 3 + 3 * (pairs - 1), *piece),
             dma((stripes + members - 1,)),
             dma, dma((chunks,)),
             dma, dma, dma, dma((chunks,)),
             dma, dma((chunks,)),
-            dma, dma((chunks,)),
+            dma,
             dma, dma, dma((chunks,)),
             dma, dma((chunks,)),
         ]

time: 78 us -> 74.6 us (0.956)
  Pallas kernels: 76.4 us -> 73.1 us
    pallas_call x1, Pallas kernels: 76.4 us -> 73.1 us  [body(): pl.pallas_call(functools.partial(kernel, groups, members), out_shape=pltp...]
where the time goes in v4:
time: 74.6 us; the launch traced here: 74.5 us
  Pallas kernels  73.1 us (98%)
    pallas_call x1, Pallas kernels, body(): pl.pallas_call(functools.partial(kernel, groups, members), out_shape=pltp...  73.1 us

profile of v4, /device:TPU:0, one launch (start us, length us, event | category | flops | bytes accessed | tf_op | source)
XLA Modules:
  0.0 74.5 jit_solution(17076999316529167592)
XLA Ops:
  0.7 73.1 %shard_map.55 = f32[4,64,256]{2,1,0:T(8,128)S(1)} custom-call(f32[4,4]{1,0:T(4,128)} %coef_ref.1, s32[4]{0:T(128)} %group_ref.1, s32[4,8]{1,0:T(4,128)} %member_ref.1, s32[1,1]{1,0:T(1,128)S(6)} %copy.8.active_ref, f32[8,8,64,1024]{3,2,1,0:T(8,128)} %bitcast.1), custom_call_target="tpu_custom_call" | custom-call | tf_op jit(solution)/shard_map/pallas_call | solution.py:388
  73.8 0.7 copy.7

commit v5 on v4

--- a/solution.py
+++ b/solution.py
@@ -23,6 +23,7 @@
     chunks, _, rows, width = tloc.shape
     stripes, samples, _, _, _ = vol.shape
     halves = chunks // stripes
+    group_of = chunks // 2
     part = width // groups
     group_cols = part * halves
     chips = members // 2
@@ -208,13 +209,16 @@
         def to_group(n):
             off = far_first(n)
             k = (g + 1 + off) % groups
-            send(tout.at[i, k], tpin.at[i, off], p_send, p_recv.at[i], {"grp": k})
+            send(tout.at[i, k], tpin.at[i, off], p_send, p_recv.at[i // group_of], {"grp": k})
         each(groups - 1, to_group)
         inbox[i, from_chip + chips - 1] = rout[i, chip]
         tpin[i, groups - 1] = tout[i, g]
 
     def factors(i):
-        landed(tpin.at[i, pl.ds(0, groups - 1)], p_recv.at[i])
+        @pl.when(i % group_of == 0)
+        def _():
+            landed(tpin.at[pl.ds(i, group_of), pl.ds(0, groups - 1)], p_recv.at[i // group_of])
+
         t = [tpin[i, e, 0] for e in range(groups)]
         total = t[0]
         for e in range(1, groups):
@@ -380,7 +384,7 @@
             dma((stripes + members - 1,)),
             dma, dma((chunks,)),
             dma, dma, dma, dma((chunks,)),
-            dma, dma((chunks,)),
+            dma, dma((2,)),
             dma,
             dma, dma, dma((chunks,)),
             dma, dma((chunks,)),

time: 74.6 us -> 74.5 us (level)
  no operation moved by 1% of the time
where the time goes in v5:
time: 74.5 us; the launch traced here: 74.4 us
  Pallas kernels  73 us (98%)
    pallas_call x1, Pallas kernels, body(): pl.pallas_call(functools.partial(kernel, groups, members), out_shape=pltp...  73 us

profile of v5, /device:TPU:0, one launch (start us, length us, event | category | flops | bytes accessed | tf_op | source)
XLA Modules:
  0.0 74.4 jit_solution(12188387169421349356)
XLA Ops:
  0.7 73.0 %shard_map.55 = f32[4,64,256]{2,1,0:T(8,128)S(1)} custom-call(f32[4,4]{1,0:T(4,128)} %coef_ref.1, s32[4]{0:T(128)} %group_ref.1, s32[4,8]{1,0:T(4,128)} %member_ref.1, s32[1,1]{1,0:T(1,128)S(6)} %copy.8.active_ref, f32[8,8,64,1024]{3,2,1,0:T(8,128)} %bitcast.1), custom_call_target="tpu_custom_call" | custom-call | tf_op jit(solution)/shard_map/pallas_call | solution.py:392
  73.7 0.7 copy.7
